TPU v7x, 512 devices: a whole 4x8x8 slice. The times are simulated.
512 devices in a mesh: gx: 64 (over y, x, core), gz: 8 (over z).
Axes of the slice: x: 4, y: 8, z: 8, core: 2. Of those that a mesh axis runs over, the one named last changes fastest.
Arguments:
- velocity: bfloat16 [3, 32, 512, 64, 128], P(None, None, 'gx', 'gz'), may hold values from -16 to 16
- weights: float32 [512, 64, 128], P('gx', 'gz'), may hold values from 1 to 60
Outputs:
- modes: float32 [3, 32, 512, 64, 128], P(None, None, 'gx', 'gz')
All inputs are finite; a program needn't handle non-finite values.
Results may differ from a plain program's by a relative error of at most 0.0003.
Values may be sent and summed in bfloat16 or wider, within the bound.
A program may use at most 64 MiB of HBM per device.

v0:
```python
import jax
import jax.numpy as jnp
from jax import lax
from jax.sharding import PartitionSpec as P

COEFS = (0.8, -0.2, 4.0 / 105.0, -1.0 / 280.0)


def extended_2(cells, sides, width):
    for axis, dim in sides:
        count = lax.axis_size(axis)
        head = lax.slice_in_dim(cells, 0, width, axis=dim)
        tail = lax.slice_in_dim(cells, cells.shape[dim] - width, cells.shape[dim], axis=dim)
        cells = jnp.concatenate(
            [
                lax.ppermute(tail, axis, [(i, (i + 1) % count) for i in range(count)]),
                cells,
                lax.ppermute(head, axis, [((i + 1) % count, i) for i in range(count)]),
            ],
            axis=dim,
        )
    return cells


def taps(extended, axis, length):
    total = None
    for step, weight in enumerate(COEFS, start=1):
        upper = lax.slice_in_dim(extended, 4 + step, 4 + step + length, axis=axis)
        lower = lax.slice_in_dim(extended, 4 - step, 4 - step + length, axis=axis)
        term = weight * (upper - lower)
        total = term if total is None else total + term
    return total


def walled(field):
    padded = jnp.pad(field, ((0, 0), (0, 0), (0, 0), (4, 4)))
    return taps(padded, 3, field.shape[3])


def per_device(velocity, weights):
    snaps = velocity.shape[1]
    cells_x = velocity.shape[2]
    cells_z = velocity.shape[3]
    cells_y = velocity.shape[4]
    whole_ext = extended_2(velocity, (("gx", 2), ("gz", 3)), 4)
    v_stream = whole_ext[1, :, :, 4 : 4 + cells_z].astype(jnp.float32)
    w_stream = whole_ext[2, :, :, 4 : 4 + cells_z].astype(jnp.float32)
    u_span = whole_ext[0, :, 4 : 4 + cells_x].astype(jnp.float32)
    v_span = whole_ext[1, :, 4 : 4 + cells_x].astype(jnp.float32)
    inner_u = velocity[0].astype(jnp.float32)
    inner_w = velocity[2].astype(jnp.float32)
    omega_x = walled(inner_w) - taps(v_span, 2, cells_z)
    omega_y = taps(u_span, 2, cells_z) - taps(w_stream, 1, cells_x)
    omega_z = taps(v_stream, 1, cells_x) - walled(inner_u)
    vort = jnp.stack([omega_x, omega_y, omega_z])
    local_gram = lax.dot_general(
        vort * weights[None, None],
        vort,
        (((0, 2, 3, 4), (0, 2, 3, 4)), ((), ())),
        precision=lax.Precision.HIGHEST,
        preferred_element_type=jnp.float32,
    )
    factor = jnp.linalg.cholesky(lax.psum(local_gram, ("gx", "gz")))
    inverse = jax.scipy.linalg.solve_triangular(
        factor, jnp.eye(snaps, dtype=jnp.float32), lower=True
    )
    rows_all = 3 * cells_x * cells_y * cells_z * lax.axis_size("gx") * lax.axis_size("gz")
    scale_all = jnp.sqrt(jnp.float32(rows_all))
    mixed = jnp.einsum("ij,cjxzy->cixzy", inverse, vort, precision=lax.Precision.HIGHEST)
    return mixed * scale_all


def solution(mesh):
    placed = (P(None, None, "gx", "gz", None), P("gx", "gz", None))
    return jax.shard_map(
        per_device,
        mesh=mesh,
        in_specs=placed,
        out_specs=P(None, None, "gx", "gz", None),
        check_vma=False,
    )
```

profile of v0, /device:TPU:1, one launch (start us, length us, event | category | flops | bytes accessed | tf_op | source)
XLA Modules:
  0.0 188.6 jit_solution(6746897384506120188)
XLA Ops:
  0.0 2.4 %copy.3 = bf16[3,32,8,8,128]{4,1,3,2,0:T(8,128)(2,1)S(1)} copy(bf16[3,32,8,8,128]{4,3,2,1,0:T(8,128)(2,1)} %param.2) | data formatting | bytes 3145728 | tf_op args[0]
  2.4 0.0 copy-start
  2.4 0.3 fusion.66
  2.8 4.6 %collective-permute-start = (bf16[3,32,4,8,128]{4,1,3,2,0:T(8,128)(2,1)S(1)}, bf16[3,32,4,8,128]{4,1,3,2,0:T(8,128)(2,1)S(1)}, u32[]{:S(2)}, u32[]{:S(2)}) collective-permute-start(bf16[3,32,4,8,128]{4,1,3,2,0:T(8,128)(2,1)S(1)} %get-tuple-element.14), channel_id=1, source_target_pairs={{0,8},{8,16},{16,24},{24,32},{32,40},{40,48},{48,56},{56,64},{64,7... | collective-permute-start | bytes 2359304 | tf_op jit(solution)/shard_map/ppermute | solution.py:16
  7.4 6.2 %collective-permute-start.1 = (bf16[3,32,4,8,128]{4,1,3,2,0:T(8,128)(2,1)S(1)}, bf16[3,32,4,8,128]{4,1,3,2,0:T(8,128)(2,1)S(1)}, u32[]{:S(2)}, u32[]{:S(2)}) collective-permute-start(bf16[3,32,4,8,128]{4,1,3,2,0:T(8,128)(2,1)S(1)} %get-tuple-element.13), channel_id=1, source_target_pairs={{8,0},{16,8},{24,16},{32,24},{40,32},{48,40},{56,48},{64,56},{72,6... | collective-permute-start | bytes 2359304 | tf_op jit(solution)/shard_map/ppermute | solution.py:18
  13.6 2.7 %collective-permute-done = bf16[3,32,4,8,128]{4,1,3,2,0:T(8,128)(2,1)S(1)} collective-permute-done((bf16[3,32,4,8,128]{4,1,3,2,0:T(8,128)(2,1)S(1)}, bf16[3,32,4,8,128]{4,1,3,2,0:T(8,128)(2,1)S(1)}, u32[]{:S(2)}, u32[]{:S(2)}) %collective-permute-start) | collective-permute-done | bytes 786464 | tf_op jit(solution)/shard_map/ppermute | solution.py:16
  16.3 0.1 constant_dynamic-update-slice_fusion.2
  16.4 0.0 copy-done
  16.4 1.1 constant_dynamic-update-slice_fusion.1
  17.5 3.5 %collective-permute-done.1 = bf16[3,32,4,8,128]{4,1,3,2,0:T(8,128)(2,1)S(1)} collective-permute-done((bf16[3,32,4,8,128]{4,1,3,2,0:T(8,128)(2,1)S(1)}, bf16[3,32,4,8,128]{4,1,3,2,0:T(8,128)(2,1)S(1)}, u32[]{:S(2)}, u32[]{:S(2)}) %collective-permute-start.1) | collective-permute-done | bytes 786464 | tf_op jit(solution)/shard_map/ppermute | solution.py:18
  21.0 0.1 constant_dynamic-update-slice_fusion
  21.1 1.0 fusion.65
  22.2 3.7 %collective-permute-start.2 = (bf16[3,32,16,4,128]{4,1,3,2,0:T(8,128)(2,1)S(1)}, bf16[3,32,16,4,128]{4,1,3,2,0:T(8,128)(2,1)S(1)}, u32[]{:S(2)}, u32[]{:S(2)}) collective-permute-start(bf16[3,32,16,4,128]{4,1,3,2,0:T(8,128)(2,1)S(1)} %get-tuple-element.7), channel_id=1, source_target_pairs={{0,1},{1,2},{2,3},{3,4},{4,5},{5,6},{6,7},{7,0},{8,9},{9,10},{10,1... | collective-permute-start | bytes 4718600 | tf_op jit(solution)/shard_map/ppermute | solution.py:16
  25.9 8.6 %collective-permute-start.3 = (bf16[3,32,16,4,128]{4,1,3,2,0:T(8,128)(2,1)S(1)}, bf16[3,32,16,4,128]{4,1,3,2,0:T(8,128)(2,1)S(1)}, u32[]{:S(2)}, u32[]{:S(2)}) collective-permute-start(bf16[3,32,16,4,128]{4,1,3,2,0:T(8,128)(2,1)S(1)} %get-tuple-element.8), channel_id=1, source_target_pairs={{1,0},{2,1},{3,2},{4,3},{5,4},{6,5},{7,6},{0,7},{9,8},{10,9},{11,1... | collective-permute-start | bytes 4718600 | tf_op jit(solution)/shard_map/ppermute | solution.py:18
  34.5 0.1 slice_bitcast_fusion.3
  34.6 0.7 pad_convert_fusion
  35.3 0.6 fusion.33
  35.9 2.1 %fusion.10 = f32[1,32,8,8,128]{4,1,3,2,0:T(8,128)S(1)} fusion(f32[32,8,8,136]{3,0,2,1:T(8,128)S(1)} %get-tuple-element.15, f32[32,16,8,128]{3,0,2,1:T(8,128)S(1)} %get-tuple-element.10), kind=kLoop, calls=%fused_computation.12 | loop fusion | flops 6029312 | bytes 17825792 | tf_op jit(solution)/shard_map/stack | solution.py:55
  37.9 27.2 %collective-permute-done.2 = bf16[3,32,16,4,128]{4,1,3,2,0:T(8,128)(2,1)S(1)} collective-permute-done((bf16[3,32,16,4,128]{4,1,3,2,0:T(8,128)(2,1)S(1)}, bf16[3,32,16,4,128]{4,1,3,2,0:T(8,128)(2,1)S(1)}, u32[]{:S(2)}, u32[]{:S(2)}) %collective-permute-start.2) | collective-permute-done | bytes 1572896 | tf_op jit(solution)/shard_map/ppermute | solution.py:16
  65.1 0.9 collective-permute-done.3
  66.0 0.3 fusion.52
  66.4 2.1 %fusion.27 = f32[1,32,8,8,128]{4,1,3,2,0:T(8,128)S(1)} fusion(f32[32,16,8,128]{3,0,2,1:T(8,128)S(1)} %get-tuple-element.9, f32[32,8,16,128]{3,0,2,1:T(8,128)S(1)} %get-tuple-element.6), kind=kLoop, calls=%fused_computation.38 | loop fusion | flops 6029312 | bytes 17825792 | tf_op jit(solution)/shard_map/stack | solution.py:55
  68.5 0.0 copy-start.1
  68.5 2.1 %fusion.46 = f32[1,32,8,8,128]{4,1,3,2,0:T(8,128)S(1)} fusion(f32[32,8,16,128]{3,0,2,1:T(8,128)S(1)} %get-tuple-element.5, f32[32,8,8,136]{3,0,2,1:T(8,128)S(1)} %get-tuple-element.16), kind=kLoop, calls=%fused_computation.68 | loop fusion | flops 6029312 | bytes 17825792 | tf_op jit(solution)/shard_map/stack | solution.py:55
  70.6 0.0 copy-done.1
  70.6 2.8 %fusion.4 = f32[32,32]{0,1:T(8,128)S(1)} fusion(f32[1,32,8,8,128]{4,1,3,2,0:T(8,128)S(1)} %fusion.10, f32[1,32,8,8,128]{4,1,3,2,0:T(8,128)S(1)} %fusion.27, f32[1,32,8,8,128]{4,1,3,2,0:T(8,128)S(1)} %fusion.46, f32[8,8,128]{2,1,0:T(8,128)S(1)} %copy-done.1), kind=kOutput, calls=%fused_computation.6 | convolution fusion | flops 305922048 | bytes 3182592 | tf_op jit(solution)/shard_map/dot_general | solution.py:56
  73.4 101.7 %psum.7 = f32[32,32]{0,1:T(8,128)S(1)} all-reduce(f32[32,32]{0,1:T(8,128)S(1)} %fusion.4), channel_id=1, replica_groups=mesh['gx'=64,'gz'=8] {'gx','gz'}, use_global_device_ids=true, to_apply=%region_0.1 | all-reduce | flops 1024 | bytes 8192 | tf_op jit(solution)/shard_map/psum | solution.py:63
  175.1 0.1 copy.9
  175.2 2.9 %cholesky.17 = f32[32,32]{1,0:T(8,128)S(1)} custom-call(f32[32,32]{1,0:T(8,128)S(1)} %fusion.62), custom_call_target="Cholesky" | custom-call | tf_op jit(solution)/shard_map/jit(cholesky)/cholesky | solution.py:63
  178.2 0.6 compare_reduce_fusion
  178.8 0.7 fusion.60
  179.5 2.4 %custom-call.7 = f32[1,32,32]{1,2,0:T(8,128)S(1)} custom-call(f32[1,32,32]{2,1,0:T(8,128)S(1)} %fusion.60), custom_call_target="InvertDiagBlocksLowerTriangular" | custom-call | tf_op jit(solution)/shard_map/jit(_solve_triangular)/triangular_solve | solution.py:64
  181.9 0.2 convolution_bitcast_fusion
  182.1 3.0 %multiply_bitcast_fusion = f32[3,32,8,8,128]{4,1,3,2,0:T(8,128)S(1)} fusion(f32[32,32,1,1,1]{1,0,4,3,2:T(8,128)S(1)} %convolution_bitcast_fusion, f32[1,32,8,8,128]{4,1,3,2,0:T(8,128)S(1)} %fusion.10, f32[1,32,8,8,128]{4,1,3,2,0:T(8,128)S(1)} %fusion.27, f32[1,32,8,8,128]{4,1,3,2,0:T(8,128)S(1)} %fusion.46), kind=kOutput, calls=%fused_computation.3 | convolution fusion | flops 304349184 | bytes 6295552 | tf_op jit(solution)/shard_map/ij,cjxzy->cixzy/dot_general | solution.py:69
  185.1 3.5 %copy.10 = f32[3,32,8,8,128]{4,3,2,1,0:T(8,128)} copy(f32[3,32,8,8,128]{4,1,3,2,0:T(8,128)S(1)} %multiply_bitcast_fusion) | data formatting | bytes 6291456 | tf_op jit(solution)/shard_map/mul | solution.py:70
  (2 shorter events, 0.0 us)
Async XLA Ops:
  2.4 14.0 %copy-start = (bf16[3,32,8,8,128]{4,3,2,1,0:T(8,128)(2,1)S(1)}, bf16[3,32,8,8,128]{4,3,2,1,0:T(8,128)(2,1)}, u32[]{:S(2)}) copy-start(bf16[3,32,8,8,128]{4,3,2,1,0:T(8,128)(2,1)} %param.2) | copy-start | bytes 4718596
  2.8 13.6 %collective-permute-start = (bf16[3,32,4,8,128]{4,1,3,2,0:T(8,128)(2,1)S(1)}, bf16[3,32,4,8,128]{4,1,3,2,0:T(8,128)(2,1)S(1)}, u32[]{:S(2)}, u32[]{:S(2)}) collective-permute-start(bf16[3,32,4,8,128]{4,1,3,2,0:T(8,128)(2,1)S(1)} %get-tuple-element.14), channel_id=1, source_target_pairs={{0,8},{8,16},{16,24},{24,32},{32,40},{40,48},{48,56},{56,64},{64,7... | collective-permute-start | bytes 2359304 | tf_op jit(solution)/shard_map/ppermute | solution.py:16
  7.4 13.6 %collective-permute-start.1 = (bf16[3,32,4,8,128]{4,1,3,2,0:T(8,128)(2,1)S(1)}, bf16[3,32,4,8,128]{4,1,3,2,0:T(8,128)(2,1)S(1)}, u32[]{:S(2)}, u32[]{:S(2)}) collective-permute-start(bf16[3,32,4,8,128]{4,1,3,2,0:T(8,128)(2,1)S(1)} %get-tuple-element.13), channel_id=1, source_target_pairs={{8,0},{16,8},{24,16},{32,24},{40,32},{48,40},{56,48},{64,56},{72,6... | collective-permute-start | bytes 2359304 | tf_op jit(solution)/shard_map/ppermute | solution.py:18
  22.2 43.0 %collective-permute-start.2 = (bf16[3,32,16,4,128]{4,1,3,2,0:T(8,128)(2,1)S(1)}, bf16[3,32,16,4,128]{4,1,3,2,0:T(8,128)(2,1)S(1)}, u32[]{:S(2)}, u32[]{:S(2)}) collective-permute-start(bf16[3,32,16,4,128]{4,1,3,2,0:T(8,128)(2,1)S(1)} %get-tuple-element.7), channel_id=1, source_target_pairs={{0,1},{1,2},{2,3},{3,4},{4,5},{5,6},{6,7},{7,0},{8,9},{9,10},{10,1... | collective-permute-start | bytes 4718600 | tf_op jit(solution)/shard_map/ppermute | solution.py:16
  25.9 40.1 %collective-permute-start.3 = (bf16[3,32,16,4,128]{4,1,3,2,0:T(8,128)(2,1)S(1)}, bf16[3,32,16,4,128]{4,1,3,2,0:T(8,128)(2,1)S(1)}, u32[]{:S(2)}, u32[]{:S(2)}) collective-permute-start(bf16[3,32,16,4,128]{4,1,3,2,0:T(8,128)(2,1)S(1)} %get-tuple-element.8), channel_id=1, source_target_pairs={{1,0},{2,1},{3,2},{4,3},{5,4},{6,5},{7,6},{0,7},{9,8},{10,9},{11,1... | collective-permute-start | bytes 4718600 | tf_op jit(solution)/shard_map/ppermute | solution.py:18
  68.5 2.1 %copy-start.1 = (f32[8,8,128]{2,1,0:T(8,128)S(1)}, f32[8,8,128]{2,1,0:T(8,128)}, u32[]{:S(2)}) copy-start(f32[8,8,128]{2,1,0:T(8,128)} %param.3) | copy-start | bytes 98308
where the time goes:
time: 189 us
  blocking collectives  102 us (54%)
  waiting for transfers between devices  34.3 us (18%)
  starting transfers between devices  23.1 us (12%)
  other arithmetic  14.6 us (8%)
  local copies, waits for them, and re-layouts  8.7 us (5%)
  matrix products  6.01 us (3%)
    psum x1, blocking collectives, per_device(): factor = jnp.linalg.cholesky(lax.psum(local_gram, ('gx', 'gz')))  102 us
    ppermute x2, waiting for transfers between devices, extended_2(): lax.ppermute(tail, axis, [(i, (i + 1) % count) for i in range(count)])  29.9 us
    ppermute x2, starting transfers between devices, extended_2(): lax.ppermute(head, axis, [((i + 1) % count, i) for i in range(count)])  14.8 us
    ppermute x2, starting transfers between devices, extended_2(): lax.ppermute(tail, axis, [(i, (i + 1) % count) for i in range(count)])  8.35 us
    another operation x3, other arithmetic, per_device(): vort = jnp.stack([omega_x, omega_y, omega_z])  6.27 us
    ppermute x2, waiting for transfers between devices, extended_2(): lax.ppermute(head, axis, [((i + 1) % count, i) for i in range(count)])  4.41 us
  transfers between devices with their start and end apart: 4, of which 4 were waited for; matrix products, arithmetic and copies ran while one was open for 2% of the time, Pallas kernels for 0%

commit v1 on v0

--- a/solution.py
+++ b/solution.py
@@ -1,9 +1,20 @@
+import functools
 import jax
 import jax.numpy as jnp
 from jax import lax
 from jax.sharding import PartitionSpec as P
+from jax.lax import all_gather
 
 COEFS = (0.8, -0.2, 4.0 / 105.0, -1.0 / 280.0)
+
+
+def column_process(inputs, which_axis):
+    local_now = all_gather(inputs, axis_name=which_axis)
+    parts_out = jnp.sum(local_now, axis=0)
+    return parts_out
+
+
+supply_series = functools.partial(column_process, which_axis=("gx", "gz"))
 
 
 def extended_2(cells, sides, width):
@@ -60,7 +71,7 @@
         precision=lax.Precision.HIGHEST,
         preferred_element_type=jnp.float32,
     )
-    factor = jnp.linalg.cholesky(lax.psum(local_gram, ("gx", "gz")))
+    factor = jnp.linalg.cholesky(supply_series(local_gram))
     inverse = jax.scipy.linalg.solve_triangular(
         factor, jnp.eye(snaps, dtype=jnp.float32), lower=True
     )

time: 189 us -> 235 us (1.24)
  waiting for transfers between devices: 34.3 us -> 164 us
  blocking collectives: 102 us -> 0 us
  between operations: 0.18 us -> 13.6 us
  other arithmetic: 14.6 us -> 18.7 us
    all_gather x0 -> x1, waiting for transfers between devices: none -> 130 us  [column_process(): local_now = all_gather(inputs, axis_name=which_axis)]
    psum x1 -> x0, blocking collectives: 102 us -> none  [per_device(): factor = jnp.linalg.cholesky(lax.psum(local_gram, ('gx', 'gz')))]
    reduce_sum x0 -> x1, other arithmetic: none -> 3.99 us  [column_process(): parts_out = jnp.sum(local_now, axis=0)]
  transfers between devices with their start and end apart: 4 -> 5, of which waited for: 4 -> 5; matrix products, arithmetic and copies ran while one was open for 2% -> 2% of each run, Pallas kernels for 0% -> 0%
where the time goes in v1:
time: 235 us
  waiting for transfers between devices  164 us (70%)
  starting transfers between devices  23.1 us (10%)
  other arithmetic  18.7 us (8%)
  between operations  13.6 us (6%)
  local copies, waits for them, and re-layouts  8.7 us (4%)
  matrix products  6.57 us (3%)
    all_gather x1, waiting for transfers between devices, column_process(): local_now = all_gather(inputs, axis_name=which_axis)  130 us
    ppermute x2, waiting for transfers between devices, extended_2(): lax.ppermute(tail, axis, [(i, (i + 1) % count) for i in range(count)])  29.9 us
    ppermute x2, starting transfers between devices, extended_2(): lax.ppermute(head, axis, [((i + 1) % count, i) for i in range(count)])  14.8 us
    ppermute x2, starting transfers between devices, extended_2(): lax.ppermute(tail, axis, [(i, (i + 1) % count) for i in range(count)])  8.35 us
    another operation x3, other arithmetic, per_device(): vort = jnp.stack([omega_x, omega_y, omega_z])  6.45 us
  transfers between devices with their start and end apart: 5, of which 5 were waited for; matrix products, arithmetic and copies ran while one was open for 2% of the time, Pallas kernels for 0%

profile of v1, /device:TPU:1, one launch (start us, length us, event | category | flops | bytes accessed | tf_op | source)
XLA Modules:
  0.0 234.6 jit_solution(14224738332593391067)
XLA Ops:
  6.5 0.0 all-gather.3.cloned.1.call-start
  6.5 2.4 %copy.10 = bf16[3,32,8,8,128]{4,1,3,2,0:T(8,128)(2,1)S(1)} copy(bf16[3,32,8,8,128]{4,3,2,1,0:T(8,128)(2,1)} %param.2) | data formatting | bytes 3145728 | tf_op args[0]
  9.0 0.0 copy-start
  9.0 0.3 fusion.66
  9.3 4.6 %collective-permute-start = (bf16[3,32,4,8,128]{4,1,3,2,0:T(8,128)(2,1)S(1)}, bf16[3,32,4,8,128]{4,1,3,2,0:T(8,128)(2,1)S(1)}, u32[]{:S(2)}, u32[]{:S(2)}) collective-permute-start(bf16[3,32,4,8,128]{4,1,3,2,0:T(8,128)(2,1)S(1)} %get-tuple-element.14), channel_id=1, source_target_pairs={{0,8},{8,16},{16,24},{24,32},{32,40},{40,48},{48,56},{56,64},{64,7... | collective-permute-start | bytes 2359304 | tf_op jit(solution)/shard_map/ppermute | solution.py:27
  14.0 6.2 %collective-permute-start.1 = (bf16[3,32,4,8,128]{4,1,3,2,0:T(8,128)(2,1)S(1)}, bf16[3,32,4,8,128]{4,1,3,2,0:T(8,128)(2,1)S(1)}, u32[]{:S(2)}, u32[]{:S(2)}) collective-permute-start(bf16[3,32,4,8,128]{4,1,3,2,0:T(8,128)(2,1)S(1)} %get-tuple-element.13), channel_id=1, source_target_pairs={{8,0},{16,8},{24,16},{32,24},{40,32},{48,40},{56,48},{64,56},{72,6... | collective-permute-start | bytes 2359304 | tf_op jit(solution)/shard_map/ppermute | solution.py:29
  20.2 2.7 %collective-permute-done = bf16[3,32,4,8,128]{4,1,3,2,0:T(8,128)(2,1)S(1)} collective-permute-done((bf16[3,32,4,8,128]{4,1,3,2,0:T(8,128)(2,1)S(1)}, bf16[3,32,4,8,128]{4,1,3,2,0:T(8,128)(2,1)S(1)}, u32[]{:S(2)}, u32[]{:S(2)}) %collective-permute-start) | collective-permute-done | bytes 786464 | tf_op jit(solution)/shard_map/ppermute | solution.py:27
  22.9 0.1 constant_dynamic-update-slice_fusion.2
  22.9 0.0 copy-done
  22.9 1.1 constant_dynamic-update-slice_fusion.1
  24.1 3.5 %collective-permute-done.1 = bf16[3,32,4,8,128]{4,1,3,2,0:T(8,128)(2,1)S(1)} collective-permute-done((bf16[3,32,4,8,128]{4,1,3,2,0:T(8,128)(2,1)S(1)}, bf16[3,32,4,8,128]{4,1,3,2,0:T(8,128)(2,1)S(1)}, u32[]{:S(2)}, u32[]{:S(2)}) %collective-permute-start.1) | collective-permute-done | bytes 786464 | tf_op jit(solution)/shard_map/ppermute | solution.py:29
  27.6 0.1 constant_dynamic-update-slice_fusion
  27.7 1.0 fusion.65
  28.7 3.7 %collective-permute-start.2 = (bf16[3,32,16,4,128]{4,1,3,2,0:T(8,128)(2,1)S(1)}, bf16[3,32,16,4,128]{4,1,3,2,0:T(8,128)(2,1)S(1)}, u32[]{:S(2)}, u32[]{:S(2)}) collective-permute-start(bf16[3,32,16,4,128]{4,1,3,2,0:T(8,128)(2,1)S(1)} %get-tuple-element.7), channel_id=1, source_target_pairs={{0,1},{1,2},{2,3},{3,4},{4,5},{5,6},{6,7},{7,0},{8,9},{9,10},{10,1... | collective-permute-start | bytes 4718600 | tf_op jit(solution)/shard_map/ppermute | solution.py:27
  32.4 8.6 %collective-permute-start.3 = (bf16[3,32,16,4,128]{4,1,3,2,0:T(8,128)(2,1)S(1)}, bf16[3,32,16,4,128]{4,1,3,2,0:T(8,128)(2,1)S(1)}, u32[]{:S(2)}, u32[]{:S(2)}) collective-permute-start(bf16[3,32,16,4,128]{4,1,3,2,0:T(8,128)(2,1)S(1)} %get-tuple-element.8), channel_id=1, source_target_pairs={{1,0},{2,1},{3,2},{4,3},{5,4},{6,5},{7,6},{0,7},{9,8},{10,9},{11,1... | collective-permute-start | bytes 4718600 | tf_op jit(solution)/shard_map/ppermute | solution.py:29
  41.0 0.1 slice_bitcast_fusion.3
  41.1 0.7 pad_convert_fusion
  41.8 0.6 fusion.33
  42.4 2.1 fusion.10
  44.5 27.2 %collective-permute-done.2 = bf16[3,32,16,4,128]{4,1,3,2,0:T(8,128)(2,1)S(1)} collective-permute-done((bf16[3,32,16,4,128]{4,1,3,2,0:T(8,128)(2,1)S(1)}, bf16[3,32,16,4,128]{4,1,3,2,0:T(8,128)(2,1)S(1)}, u32[]{:S(2)}, u32[]{:S(2)}) %collective-permute-start.2) | collective-permute-done | bytes 1572896 | tf_op jit(solution)/shard_map/ppermute | solution.py:27
  71.7 0.9 collective-permute-done.3
  72.6 0.3 fusion.52
  72.9 2.1 fusion.27
  75.0 0.0 copy-start.1
  75.0 2.2 fusion.46
  77.3 0.0 copy-done.1
  77.3 3.4 %fusion.4 = f32[32,32]{1,0:T(8,128)} fusion(f32[1,32,8,8,128]{4,1,3,2,0:T(8,128)S(1)} %fusion.10, f32[1,32,8,8,128]{4,1,3,2,0:T(8,128)S(1)} %fusion.27, f32[1,32,8,8,128]{4,1,3,2,0:T(8,128)S(1)} %fusion.46, f32[8,8,128]{2,1,0:T(8,128)S(1)} %copy-done.1), kind=kOutput, calls=%fused_computation.6 | convolution fusion | flops 305922048 | bytes 3182592 | tf_op jit(solution)/shard_map/dot_general | solution.py:67
  80.7 0.0 all-gather.3.cloned.1.call-update
  80.7 129.6 %all-gather.3.cloned.1.call-done = f32[16384,32]{1,0:T(8,128)} async-done(((f32[32,32]{1,0:T(8,128)}), f32[16384,32]{1,0:T(8,128)}) %all-gather.3.cloned.1.call-update) | async-done | bytes 2097168 | tf_op jit(solution)/shard_map/all_gather | solution.py:12
  210.3 4.0 %reduce_sum.9 = f32[32,32]{1,0:T(8,128)S(1)} reduce(f32[512,32,32]{2,1,0:T(8,128)} %bitcast.51, f32[]{:T(128)} %constant.53.clone.1), dimensions={0}, to_apply=%region_0.1 | reduce | flops 523264 | bytes 2101252 | tf_op jit(solution)/shard_map/reduce_sum | solution.py:13
  214.3 0.1 copy.15
  214.4 2.9 %cholesky.17 = f32[32,32]{1,0:T(8,128)S(1)} custom-call(f32[32,32]{1,0:T(8,128)S(1)} %fusion.62), custom_call_target="Cholesky" | custom-call | tf_op jit(solution)/shard_map/jit(cholesky)/cholesky | solution.py:74
  217.3 0.6 compare_reduce_fusion
  218.0 0.7 fusion.60
  218.6 2.4 %custom-call.7 = f32[1,32,32]{1,2,0:T(8,128)S(1)} custom-call(f32[1,32,32]{2,1,0:T(8,128)S(1)} %fusion.60), custom_call_target="InvertDiagBlocksLowerTriangular" | custom-call | tf_op jit(solution)/shard_map/jit(_solve_triangular)/triangular_solve | solution.py:75
  221.1 0.2 convolution_bitcast_fusion
  221.3 3.0 %multiply_bitcast_fusion = f32[3,32,8,8,128]{4,1,3,2,0:T(8,128)S(1)} fusion(f32[32,32,1,1,1]{1,0,4,3,2:T(8,128)S(1)} %convolution_bitcast_fusion, f32[1,32,8,8,128]{4,1,3,2,0:T(8,128)S(1)} %fusion.10, f32[1,32,8,8,128]{4,1,3,2,0:T(8,128)S(1)} %fusion.27, f32[1,32,8,8,128]{4,1,3,2,0:T(8,128)S(1)} %fusion.46), kind=kOutput, calls=%fused_computation.3 | convolution fusion | flops 304349184 | bytes 6295552 | tf_op jit(solution)/shard_map/ij,cjxzy->cixzy/dot_general | solution.py:80
  224.3 3.5 %copy.16 = f32[3,32,8,8,128]{4,3,2,1,0:T(8,128)} copy(f32[3,32,8,8,128]{4,1,3,2,0:T(8,128)S(1)} %multiply_bitcast_fusion) | data formatting | bytes 6291456 | tf_op jit(solution)/shard_map/mul | solution.py:81
  (2 shorter events, 0.0 us)
Async XLA Ops:
  6.5 203.8 %all-gather.3.cloned.1.call-start = ((), (), s32[]{:S(2)}) async-start(), calls=%async_computation | async-start | bytes 8404992 | tf_op jit(solution)/shard_map/all_gather | solution.py:12
  9.0 14.0 %copy-start = (bf16[3,32,8,8,128]{4,3,2,1,0:T(8,128)(2,1)S(1)}, bf16[3,32,8,8,128]{4,3,2,1,0:T(8,128)(2,1)}, u32[]{:S(2)}) copy-start(bf16[3,32,8,8,128]{4,3,2,1,0:T(8,128)(2,1)} %param.2) | copy-start | bytes 4718596
  9.3 13.6 %collective-permute-start = (bf16[3,32,4,8,128]{4,1,3,2,0:T(8,128)(2,1)S(1)}, bf16[3,32,4,8,128]{4,1,3,2,0:T(8,128)(2,1)S(1)}, u32[]{:S(2)}, u32[]{:S(2)}) collective-permute-start(bf16[3,32,4,8,128]{4,1,3,2,0:T(8,128)(2,1)S(1)} %get-tuple-element.14), channel_id=1, source_target_pairs={{0,8},{8,16},{16,24},{24,32},{32,40},{40,48},{48,56},{56,64},{64,7... | collective-permute-start | bytes 2359304 | tf_op jit(solution)/shard_map/ppermute | solution.py:27
  14.0 13.6 %collective-permute-start.1 = (bf16[3,32,4,8,128]{4,1,3,2,0:T(8,128)(2,1)S(1)}, bf16[3,32,4,8,128]{4,1,3,2,0:T(8,128)(2,1)S(1)}, u32[]{:S(2)}, u32[]{:S(2)}) collective-permute-start(bf16[3,32,4,8,128]{4,1,3,2,0:T(8,128)(2,1)S(1)} %get-tuple-element.13), channel_id=1, source_target_pairs={{8,0},{16,8},{24,16},{32,24},{40,32},{48,40},{56,48},{64,56},{72,6... | collective-permute-start | bytes 2359304 | tf_op jit(solution)/shard_map/ppermute | solution.py:29
  28.7 43.0 %collective-permute-start.2 = (bf16[3,32,16,4,128]{4,1,3,2,0:T(8,128)(2,1)S(1)}, bf16[3,32,16,4,128]{4,1,3,2,0:T(8,128)(2,1)S(1)}, u32[]{:S(2)}, u32[]{:S(2)}) collective-permute-start(bf16[3,32,16,4,128]{4,1,3,2,0:T(8,128)(2,1)S(1)} %get-tuple-element.7), channel_id=1, source_target_pairs={{0,1},{1,2},{2,3},{3,4},{4,5},{5,6},{6,7},{7,0},{8,9},{9,10},{10,1... | collective-permute-start | bytes 4718600 | tf_op jit(solution)/shard_map/ppermute | solution.py:27
  32.4 40.1 %collective-permute-start.3 = (bf16[3,32,16,4,128]{4,1,3,2,0:T(8,128)(2,1)S(1)}, bf16[3,32,16,4,128]{4,1,3,2,0:T(8,128)(2,1)S(1)}, u32[]{:S(2)}, u32[]{:S(2)}) collective-permute-start(bf16[3,32,16,4,128]{4,1,3,2,0:T(8,128)(2,1)S(1)} %get-tuple-element.8), channel_id=1, source_target_pairs={{1,0},{2,1},{3,2},{4,3},{5,4},{6,5},{7,6},{0,7},{9,8},{10,9},{11,1... | collective-permute-start | bytes 4718600 | tf_op jit(solution)/shard_map/ppermute | solution.py:29
  75.0 2.3 copy-start.1
Sparse Core Ops, SparseCore 0:
  80.8 129.4 all-gather.2
